TPU v7x, 128 devices: a whole 4x4x4 slice. The times are simulated.
128 devices in a mesh: pos: 2 (over y_hi), tv: 8 (over x, core), sv: 8 (over y_lo, z).
Axes of the slice: x: 4, y: 4 (y_hi: 2, y_lo: 2; y = y_hi * 2 + y_lo), z: 4, core: 2. Of those that a mesh axis runs over, the one named last changes fastest.
Arguments:
- teacher_hidden: bfloat16 [1024, 8192], P(None, 'pos')
- teacher_head: bfloat16 [8192, 81920], P('pos', ('tv', 'sv')), may hold values from -0.19824219 to 0.19824219
- align_pos: int32 [1024], replicated, may hold values from 0 to 1023, as said below
- pair_teacher: int32 [3072], P(('tv', 'sv')), may hold values from 0 to 9, as said below
- pair_student: int32 [3072], P(('tv', 'sv')), may hold values from 0 to 511, as said below
- align_values: bfloat16 [3072, 128, 128], P(('tv', 'sv'))
- student_hidden: bfloat16 [1024, 4096], P(None, 'pos')
- student_head: bfloat16 [4096, 65536], P('pos', ('tv', 'sv')), may hold values from -0.28125 to 0.28125
Outputs:
- row_loss: float32 [1024], P('pos')
- head_grad: bfloat16 [4096, 65536], P('pos', ('tv', 'sv'))
Inputs may be any that keep to these rules, and one draw needn't show every extreme that they name: `align_pos`: nondecreasing. Entry k names teacher block (k // 48) * 10 + pair_teacher[k]. `pair_student`: the student blocks b of a pair list's entries (k // 48) * 48 to (k // 48) * 48 + 47 have at most 2 entries with the same b // 8; this bound is reached.
All inputs are finite; a program needn't handle non-finite values.
Results may differ from a plain program's by a relative error of at most 0.0048.
Values may be sent and summed in bfloat16 or wider, within the bound.
No kernel may reach another device: no remote copies, remote signals or barrier semaphores. Data moves between devices by JAX's collectives and lax.ppermute only.
A program may use at most 192 MiB of HBM per device.

v0:
```python
import jax
import jax.numpy as jnp
from jax import lax
from jax.sharding import PartitionSpec as P

CAP = 2
loss_scale = 1024.0


def local(
    teacher_hidden,
    teacher_head,
    align_pos,
    pair_teacher,
    pair_student,
    align_values,
    student_hidden,
    student_head,
):
    pos_count = lax.axis_size("pos")
    owners = lax.axis_size("tv") * lax.axis_size("sv")
    own_rows = student_hidden.shape[0] // pos_count
    block_size = align_values.shape[1]
    picked = jnp.take(teacher_hidden, align_pos, axis=0)
    sliced = picked
    teacher_logits = lax.psum_scatter(
        jnp.dot(sliced, teacher_head, preferred_element_type=jnp.float32),
        "pos",
        scatter_dimension=0,
        tiled=True,
    )
    local_peak = jnp.max(teacher_logits, axis=1)
    teacher_max = lax.pmax(local_peak, ("tv", "sv"))
    teacher_total = lax.psum(
        jnp.sum(jnp.exp(teacher_logits - teacher_max[:, None]), axis=1), ("tv", "sv")
    )
    teacher_prob = (jnp.exp(teacher_logits - teacher_max[:, None]) / teacher_total[:, None]).astype(
        jnp.bfloat16
    )
    teacher_blocks = teacher_prob.reshape(own_rows, -1, block_size)
    selected = jnp.take(teacher_blocks, pair_teacher, axis=1)
    products = jnp.einsum(
        "rpk,pkn->prn", selected, align_values, preferred_element_type=jnp.float32
    ).astype(jnp.bfloat16)
    student_blocks = student_head.shape[1] // block_size
    owner_of = pair_student // student_blocks
    local_block = pair_student % student_blocks
    pair_order = jnp.arange(pair_student.shape[0], dtype=jnp.int32)
    earlier = (owner_of[None, :] == owner_of[:, None]) & (pair_order[None, :] < pair_order[:, None])
    position = jnp.sum(earlier.astype(jnp.int32), axis=1)
    slot_index = owner_of * CAP + position
    outgoing = (
        jnp.zeros((owners * CAP, own_rows, block_size), jnp.bfloat16).at[slot_index].set(products)
    )
    labels = jnp.full((owners * CAP,), -1, jnp.int32).at[slot_index].set(local_block)
    arrived, arrived_labels = (
        lax.all_to_all(
            outgoing.reshape(owners, CAP, own_rows, block_size),
            ("tv", "sv"),
            split_axis=0,
            concat_axis=0,
            tiled=True,
        ),
        lax.all_to_all(
            labels.reshape(owners, CAP), ("tv", "sv"), split_axis=0, concat_axis=0, tiled=True
        ),
    )
    arrived = arrived.reshape(owners * CAP, own_rows, block_size)
    arrived_labels = arrived_labels.reshape(owners * CAP)
    selector = (
        arrived_labels[:, None] == jnp.arange(student_blocks, dtype=jnp.int32)[None, :]
    ).astype(jnp.bfloat16)
    target = jnp.einsum(
        "sb,srn->rbn", selector, arrived, preferred_element_type=jnp.float32
    ).reshape(own_rows, -1)
    sliced = student_hidden
    student_logits = lax.psum_scatter(
        jnp.dot(sliced, student_head, preferred_element_type=jnp.float32),
        "pos",
        scatter_dimension=0,
        tiled=True,
    )
    student_local = jnp.max(student_logits, axis=1)
    mass_local = jnp.sum(target, axis=1)
    weighted_local = jnp.sum(target * student_logits, axis=1)
    student_peak = lax.pmax(student_local, ("tv", "sv"))
    spread = jnp.sum(jnp.exp(student_logits - student_peak[:, None]), axis=1)
    student_total, mass, weighted = lax.psum((spread, mass_local, weighted_local), ("tv", "sv"))
    row_loss = mass * (student_peak + jnp.log(student_total)) - weighted
    student_prob = jnp.exp(student_logits - student_peak[:, None]) / student_total[:, None]
    gradient = (loss_scale * (student_prob * mass[:, None] - target)).astype(jnp.bfloat16)
    head_grad = lax.dot_general(
        student_hidden,
        lax.all_gather(gradient, "pos", axis=0, tiled=True),
        (((0,), (0,)), ((), ())),
        preferred_element_type=jnp.float32,
    )
    return (row_loss, head_grad.astype(jnp.bfloat16))


def solution(mesh):
    placed = (
        P(None, "pos"),
        P("pos", ("tv", "sv")),
        P(),
        P(("tv", "sv")),
        P(("tv", "sv")),
        P(("tv", "sv"), None, None),
        P(None, "pos"),
        P("pos", ("tv", "sv")),
    )
    return jax.shard_map(
        local,
        mesh=mesh,
        in_specs=placed,
        out_specs=(P("pos"), P("pos", ("tv", "sv"))),
        check_vma=False,
    )
```

profile of v0, /device:TPU:1, one launch (start us, length us, event | category | flops | bytes accessed | tf_op | source)
XLA Modules:
  0.0 967.3 jit_solution(4283741941245905266)
XLA Ops:
  7.2 10.1 %fusion.28 = f32[1024,1024]{1,0:T(8,128)} fusion(bf16[1024,2048]{1,0:T(8,128)(2,1)} %param.14, bf16[2048,1024]{1,0:T(8,128)(2,1)} %param.15), kind=kOutput, calls=%fused_computation.50 | convolution fusion | flops 4294967296 | bytes 12582912 | tf_op jit(solution)/shard_map/dot_general | solution.py:78
  18.0 19.5 %gather_fusion = bf16[1024,4096]{1,0:T(8,128)(2,1)} fusion(bf16[1024,4096]{1,0:T(8,128)(2,1)} %param.8, s32[1024]{0:T(1024)S(1)} %fusion.21), kind=kCustom, calls=%fused_computation | custom fusion | bytes 16781312 | tf_op jit(solution)/shard_map/jit(_take)/gather | solution.py:24
  37.5 18.6 %fusion = f32[1024,1280]{1,0:T(8,128)} fusion(bf16[4096,1280]{1,0:T(8,128)(2,1)} %param.9, bf16[1024,4096]{1,0:T(8,128)(2,1)} %gather_fusion, pred[1024]{0:T(1024)(128)(4,1)S(1)} %compare_and_fusion), kind=kOutput, calls=%fused_computation.4 | convolution fusion | flops 10741612544 | bytes 24118272 | tf_op jit(solution)/shard_map/dot_general | solution.py:27
  58.5 10.6 %all-to-all-start.1 = ((s32[64,1,2]{2,1,0:T(1,128)}), s32[64,1,2]{2,1,0:T(1,128)S(1)}, u32[]{:S(2)}, u32[]{:S(2)}) async-start(s32[64,1,2]{2,1,0:T(1,128)} %bitcast.4), calls=%async_computation.2 | async-start | bytes 65536 | tf_op jit(solution)/shard_map/all_to_all | solution.py:64
  69.1 10.2 %reduce-scatter.5.cloned.1.call-done = f32[512,1024]{1,0:T(8,128)} async-done(((f32[1024,1024]{1,0:T(8,128)}), f32[512,1024]{1,0:T(8,128)}) %reduce-scatter.5.cloned.1.call-update) | async-done | bytes 2097168 | tf_op jit(solution)/shard_map/reduce_scatter | solution.py:77
  81.1 69.9 %reduce-scatter.3.cloned.1.call-done = f32[512,1280]{1,0:T(8,128)} async-done(((f32[1024,1280]{1,0:T(8,128)}), f32[512,1280]{1,0:T(8,128)}) %reduce-scatter.3.cloned.1.call-update) | async-done | bytes 2621456 | tf_op jit(solution)/shard_map/reduce_scatter | solution.py:26
  152.9 131.7 %all-reduce.1 = (f32[512]{0:T(512)S(1)}, f32[512]{0:T(512)S(1)}) all-reduce(f32[512]{0:T(512)S(1)} %reduce_max.19, f32[512]{0:T(512)S(1)} %reduce_max.18), channel_id=1, replica_groups=mesh['pos'=2,'tv'=8,'sv'=8] {'tv','sv'}, use_global_device_ids=true, to_apply=%region_12.13 | all-reduce | flops 1024 | bytes 8192 | tf_op jit(solution)/shard_map/pmax | solution.py:86
  284.6 2.2 fusion.12
  286.8 138.6 %psum.28 = f32[512]{0:T(512)S(1)} all-reduce(f32[512]{0:T(512)S(1)} %fusion.12), channel_id=1, replica_groups=mesh['pos'=2,'tv'=8,'sv'=8] {'tv','sv'}, use_global_device_ids=true, to_apply=%region_5.6 | all-reduce | flops 512 | bytes 4096 | tf_op jit(solution)/shard_map/psum | solution.py:34
  425.4 2.2 divide_convert_fusion
  430.9 5.0 gather_fusion.1
  435.9 7.3 fusion.8
  443.1 6.1 broadcast_in_dim.46
  449.3 16.8 %scatter_fusion = bf16[128,512,128]{2,1,0:T(8,128)(2,1)} fusion(bf16[128,512,128]{2,1,0:T(8,128)(2,1)} %broadcast_in_dim.46, s32[48]{0:T(128)S(1)} %compare_select_fusion.2, bf16[48,512,128]{2,1,0:T(8,128)(2,1)} %fusion.8), kind=kCustom, calls=%fused_computation.2 | custom fusion | bytes 18874560 | tf_op jit(solution)/shard_map/scatter | solution.py:53
  466.0 30.7 %copy.23 = bf16[64,2,512,128]{3,1,2,0:T(2,128)(2,1)} copy(bf16[64,2,512,128]{3,2,1,0:T(8,128)(2,1)} %bitcast.37) | data formatting | bytes 33554432 | tf_op jit(solution)/shard_map/reshape | solution.py:58
  496.7 17.3 %all-to-all-start = ((bf16[64,2,512,128]{3,1,2,0:T(2,128)(2,1)}), bf16[64,2,512,128]{3,1,2,0:T(2,128)(2,1)}, u32[]{:S(2)}, u32[]{:S(2)}) async-start(bf16[64,2,512,128]{3,1,2,0:T(2,128)(2,1)} %copy.23), calls=%async_computation.1 | async-start | bytes 33554432 | tf_op jit(solution)/shard_map/all_to_all | solution.py:57
  515.4 224.9 %all-to-all-done = bf16[64,2,512,128]{3,1,2,0:T(2,128)(2,1)} async-done(((bf16[64,2,512,128]{3,1,2,0:T(2,128)(2,1)}), bf16[64,2,512,128]{3,1,2,0:T(2,128)(2,1)}, u32[]{:S(2)}, u32[]{:S(2)}) %all-to-all-start) | async-done | bytes 16777248 | tf_op jit(solution)/shard_map/all_to_all | solution.py:57
  740.4 17.1 %copy.24 = bf16[64,2,512,128]{3,1,0,2:T(2,128)(2,1)S(1)} copy(bf16[64,2,512,128]{3,1,2,0:T(2,128)(2,1)} %all-to-all-done) | data formatting | bytes 33554432 | tf_op jit(solution)/shard_map/all_to_all | solution.py:57
  757.5 3.0 fusion.27
  762.6 132.8 %all-reduce = (f32[512]{0:T(512)S(1)}, f32[512]{0:T(512)S(1)}, f32[512]{0:T(512)S(1)}) all-reduce(f32[512]{0:T(512)S(1)} %get-tuple-element.11, f32[512]{0:T(512)S(1)} %get-tuple-element.19, f32[512]{0:T(512)S(1)} %get-tuple-element.10), channel_id=1, replica_groups=mesh['pos'=2,'tv'=8,'sv'=8] {'tv','sv'}, use_global_device_ids=true, to_apply=%region_16.17 | all-reduce | flops 1536 | bytes 12288 | tf_op jit(solution)/shard_map/psum | solution.py:88
  895.4 4.0 fusion.15
  900.0 44.9 %all-gather.2.cloned.1.call-done = bf16[1024,1024]{1,0:T(8,128)(2,1)} async-done(((bf16[512,1024]{1,0:T(8,128)(2,1)}), bf16[1024,1024]{1,0:T(8,128)(2,1)}) %all-gather.2.cloned.1.call-update) | async-done | bytes 2097168 | tf_op jit(solution)/shard_map/all_gather | solution.py:94
  944.9 9.4 convert_bitcast_fusion
  954.4 6.4 copy.26
  (40 shorter events, 14.2 us)
Async XLA Ops:
  7.2 428.7 %copy-start = (bf16[48,128,128]{2,1,0:T(8,128)(2,1)S(1)}, bf16[48,128,128]{2,1,0:T(8,128)(2,1)}, u32[]{:S(2)}) copy-start(bf16[48,128,128]{2,1,0:T(8,128)(2,1)} %param.13) | copy-start | bytes 4718596
  7.2 72.1 %reduce-scatter.5.cloned.1.call-start = ((), (), s32[]{:S(2)}) async-start(), calls=%async_computation.5 | async-start | bytes 6291456 | tf_op jit(solution)/shard_map/reduce_scatter | solution.py:77
  17.3 0.7 copy-start.4
  17.3 133.6 %reduce-scatter.3.cloned.1.call-start = ((), (), s32[]{:S(2)}) async-start(), calls=%async_computation.4 | async-start | bytes 7864320 | tf_op jit(solution)/shard_map/reduce_scatter | solution.py:26
  56.1 0.7 copy-start.5
  56.1 12.9 %copy-start.6 = (s32[48]{0:T(128)S(1)}, s32[48]{0:T(128)}, u32[]{:S(2)}) copy-start(s32[48]{0:T(128)} %param.11) | copy-start | bytes 580
  58.5 438.3 %all-to-all-start.1 = ((s32[64,1,2]{2,1,0:T(1,128)}), s32[64,1,2]{2,1,0:T(1,128)S(1)}, u32[]{:S(2)}, u32[]{:S(2)}) async-start(s32[64,1,2]{2,1,0:T(1,128)} %bitcast.4), calls=%async_computation.2 | async-start | bytes 65536 | tf_op jit(solution)/shard_map/all_to_all | solution.py:64
  496.7 243.6 %all-to-all-start = ((bf16[64,2,512,128]{3,1,2,0:T(2,128)(2,1)}), bf16[64,2,512,128]{3,1,2,0:T(2,128)(2,1)}, u32[]{:S(2)}, u32[]{:S(2)}) async-start(bf16[64,2,512,128]{3,1,2,0:T(2,128)(2,1)} %copy.23), calls=%async_computation.1 | async-start | bytes 33554432 | tf_op jit(solution)/shard_map/all_to_all | solution.py:57
  514.0 430.9 %all-gather.2.cloned.1.call-start = ((), (), s32[]{:S(2)}) async-start(), calls=%async_computation.6 | async-start | bytes 3145728 | tf_op jit(solution)/shard_map/all_gather | solution.py:94
  757.5 4.4 copy-start.3
  760.5 1.3 copy-start.2
  944.9 15.8 %copy-start.1 = (bf16[48,128,128]{2,1,0:T(8,128)(2,1)S(1)}, bf16[48,128,128]{2,1,0:T(8,128)(2,1)}, u32[]{:S(2)}) copy-start(bf16[48,128,128]{2,1,0:T(8,128)(2,1)} %param.13) | copy-start | bytes 4718596
Sparse Core Ops, SparseCore 0:
  17.4 61.8 reduce-scatter.4
  81.7 69.1 reduce-scatter.2
  899.6 45.3 all-gather.1
where the time goes:
time: 968 us; the launch traced here: 967 us
  blocking collectives  403 us (42%)
  waiting for transfers between devices  350 us (36%)
  local copies, waits for them, and re-layouts  110 us (11%)
  matrix products  48.4 us (5%)
  starting transfers between devices  28 us (3%)
  other arithmetic  14.5 us (1%)
  between operations  13.9 us (1%)
    all_to_all x1, waiting for transfers between devices, local(): lax.all_to_all(outgoing.reshape(owners, CAP, own_rows, block_size), ('tv'...  225 us
    psum x1, blocking collectives, local(): lax.psum(jnp.sum(jnp.exp(teacher_logits - teacher_max[:, None]), axis=1),...  139 us
    psum x1, blocking collectives, local(): lax.psum((spread, mass_local, weighted_local), ('tv', 'sv'))  133 us
    pmax x1, blocking collectives, local(): student_peak = lax.pmax(student_local, ('tv', 'sv'))  132 us
    reduce_scatter x1, waiting for transfers between devices, local(): lax.psum_scatter(jnp.dot(sliced, teacher_head, preferred_element_type=jnp...  69.9 us
    all_gather x1, waiting for transfers between devices, local(): lax.all_gather(gradient, 'pos', axis=0, tiled=True)  44.9 us
    reshape x1, local copies, waits for them, and re-layouts, local(): outgoing.reshape(owners, CAP, own_rows, block_size)  30.7 us
    gather x1, local copies, waits for them, and re-layouts, local(): picked = jnp.take(teacher_hidden, align_pos, axis=0)  19.5 us
  transfers between devices with their start and end apart: 5, of which 4 were waited for; matrix products, arithmetic and copies ran while one was open for 12% of the time, Pallas kernels for 0%

commit v1 on v0

--- a/solution.py
+++ b/solution.py
@@ -85,7 +85,9 @@
     weighted_local = jnp.sum(target * student_logits, axis=1)
     student_peak = lax.pmax(student_local, ("tv", "sv"))
     spread = jnp.sum(jnp.exp(student_logits - student_peak[:, None]), axis=1)
-    student_total, mass, weighted = lax.psum((spread, mass_local, weighted_local), ("tv", "sv"))
+    student_total, mass, weighted = lax.psum(
+        lax.psum((spread, mass_local, weighted_local), "sv"), "tv"
+    )
     row_loss = mass * (student_peak + jnp.log(student_total)) - weighted
     student_prob = jnp.exp(student_logits - student_peak[:, None]) / student_total[:, None]
     gradient = (loss_scale * (student_prob * mass[:, None] - target)).astype(jnp.bfloat16)

time: 968 us -> 864 us (0.89)
  blocking collectives: 403 us -> 307 us
    psum x1 -> x2, blocking collectives: 133 us -> 37 us  [the longest x1 24 us: local(): lax.psum(lax.psum((spread, mass_local, weighted_local), 'sv'), 'tv')]
  transfers between devices with their start and end apart: 5 -> 5, of which waited for: 4 -> 4; matrix products, arithmetic and copies ran while one was open for 12% -> 14% of each run, Pallas kernels for 0% -> 0%
where the time goes in v1:
time: 864 us; the launch traced here: 863 us
  waiting for transfers between devices  342 us (40%)
  blocking collectives  307 us (36%)
  local copies, waits for them, and re-layouts  110 us (13%)
  matrix products  48.4 us (6%)
  starting transfers between devices  28 us (3%)
  other arithmetic  14.5 us (2%)
  between operations  13.9 us (2%)
    all_to_all x1, waiting for transfers between devices, local(): lax.all_to_all(outgoing.reshape(owners, CAP, own_rows, block_size), ('tv'...  225 us
    psum x1, blocking collectives, local(): lax.psum(jnp.sum(jnp.exp(teacher_logits - teacher_max[:, None]), axis=1),...  139 us
    pmax x1, blocking collectives, local(): student_peak = lax.pmax(student_local, ('tv', 'sv'))  132 us
    reduce_scatter x1, waiting for transfers between devices, local(): lax.psum_scatter(jnp.dot(sliced, teacher_head, preferred_element_type=jnp...  69.9 us
    all_gather x1, waiting for transfers between devices, local(): lax.all_gather(gradient, 'pos', axis=0, tiled=True)  36.6 us
    reshape x1, local copies, waits for them, and re-layouts, local(): outgoing.reshape(owners, CAP, own_rows, block_size)  30.7 us
    psum x1, blocking collectives, local(): lax.psum(lax.psum((spread, mass_local, weighted_local), 'sv'), 'tv')  24 us
    gather x1, local copies, waits for them, and re-layouts, local(): picked = jnp.take(teacher_hidden, align_pos, axis=0)  19.5 us
  transfers between devices with their start and end apart: 5, of which 4 were waited for; matrix products, arithmetic and copies ran while one was open for 14% of the time, Pallas kernels for 0%

profile of v1, /device:TPU:1, one launch (start us, length us, event | category | flops | bytes accessed | tf_op | source)
XLA Modules:
  0.0 863.2 jit_solution(480191186144992148)
XLA Ops:
  7.2 10.1 %fusion.28 = f32[1024,1024]{1,0:T(8,128)} fusion(bf16[1024,2048]{1,0:T(8,128)(2,1)} %param.14, bf16[2048,1024]{1,0:T(8,128)(2,1)} %param.15), kind=kOutput, calls=%fused_computation.50 | convolution fusion | flops 4294967296 | bytes 12582912 | tf_op jit(solution)/shard_map/dot_general | solution.py:78
  18.0 19.5 %gather_fusion = bf16[1024,4096]{1,0:T(8,128)(2,1)} fusion(bf16[1024,4096]{1,0:T(8,128)(2,1)} %param.8, s32[1024]{0:T(1024)S(1)} %fusion.21), kind=kCustom, calls=%fused_computation | custom fusion | bytes 16781312 | tf_op jit(solution)/shard_map/jit(_take)/gather | solution.py:24
  37.5 18.6 %fusion = f32[1024,1280]{1,0:T(8,128)} fusion(bf16[4096,1280]{1,0:T(8,128)(2,1)} %param.9, bf16[1024,4096]{1,0:T(8,128)(2,1)} %gather_fusion, pred[1024]{0:T(1024)(128)(4,1)S(1)} %compare_and_fusion), kind=kOutput, calls=%fused_computation.4 | convolution fusion | flops 10741612544 | bytes 24118272 | tf_op jit(solution)/shard_map/dot_general | solution.py:27
  58.5 10.6 %all-to-all-start.1 = ((s32[64,1,2]{2,1,0:T(1,128)}), s32[64,1,2]{2,1,0:T(1,128)S(1)}, u32[]{:S(2)}, u32[]{:S(2)}) async-start(s32[64,1,2]{2,1,0:T(1,128)} %bitcast.4), calls=%async_computation.2 | async-start | bytes 65536 | tf_op jit(solution)/shard_map/all_to_all | solution.py:64
  69.1 10.2 %reduce-scatter.5.cloned.1.call-done = f32[512,1024]{1,0:T(8,128)} async-done(((f32[1024,1024]{1,0:T(8,128)}), f32[512,1024]{1,0:T(8,128)}) %reduce-scatter.5.cloned.1.call-update) | async-done | bytes 2097168 | tf_op jit(solution)/shard_map/reduce_scatter | solution.py:77
  81.1 69.9 %reduce-scatter.3.cloned.1.call-done = f32[512,1280]{1,0:T(8,128)} async-done(((f32[1024,1280]{1,0:T(8,128)}), f32[512,1280]{1,0:T(8,128)}) %reduce-scatter.3.cloned.1.call-update) | async-done | bytes 2621456 | tf_op jit(solution)/shard_map/reduce_scatter | solution.py:26
  152.9 131.7 %all-reduce = (f32[512]{0:T(512)S(1)}, f32[512]{0:T(512)S(1)}) all-reduce(f32[512]{0:T(512)S(1)} %reduce_max.19, f32[512]{0:T(512)S(1)} %reduce_max.18), channel_id=1, replica_groups=mesh['pos'=2,'tv'=8,'sv'=8] {'tv','sv'}, use_global_device_ids=true, to_apply=%region_13.14 | all-reduce | flops 1024 | bytes 8192 | tf_op jit(solution)/shard_map/pmax | solution.py:86
  284.6 2.2 fusion.12
  286.8 138.6 %psum.49 = f32[512]{0:T(512)S(1)} all-reduce(f32[512]{0:T(512)S(1)} %fusion.12), channel_id=1, replica_groups=mesh['pos'=2,'tv'=8,'sv'=8] {'tv','sv'}, use_global_device_ids=true, to_apply=%region_5.6 | all-reduce | flops 512 | bytes 4096 | tf_op jit(solution)/shard_map/psum | solution.py:34
  430.9 5.0 gather_fusion.1
  435.9 7.3 fusion.8
  443.1 6.1 broadcast_in_dim.46
  449.3 16.8 %scatter_fusion = bf16[128,512,128]{2,1,0:T(8,128)(2,1)} fusion(bf16[128,512,128]{2,1,0:T(8,128)(2,1)} %broadcast_in_dim.46, s32[48]{0:T(128)S(1)} %compare_select_fusion.2, bf16[48,512,128]{2,1,0:T(8,128)(2,1)} %fusion.8), kind=kCustom, calls=%fused_computation.2 | custom fusion | bytes 18874560 | tf_op jit(solution)/shard_map/scatter | solution.py:53
  466.0 30.7 %copy.23 = bf16[64,2,512,128]{3,1,2,0:T(2,128)(2,1)} copy(bf16[64,2,512,128]{3,2,1,0:T(8,128)(2,1)} %bitcast.37) | data formatting | bytes 33554432 | tf_op jit(solution)/shard_map/reshape | solution.py:58
  496.7 17.3 %all-to-all-start = ((bf16[64,2,512,128]{3,1,2,0:T(2,128)(2,1)}), bf16[64,2,512,128]{3,1,2,0:T(2,128)(2,1)}, u32[]{:S(2)}, u32[]{:S(2)}) async-start(bf16[64,2,512,128]{3,1,2,0:T(2,128)(2,1)} %copy.23), calls=%async_computation.1 | async-start | bytes 33554432 | tf_op jit(solution)/shard_map/all_to_all | solution.py:57
  515.4 224.9 %all-to-all-done = bf16[64,2,512,128]{3,1,2,0:T(2,128)(2,1)} async-done(((bf16[64,2,512,128]{3,1,2,0:T(2,128)(2,1)}), bf16[64,2,512,128]{3,1,2,0:T(2,128)(2,1)}, u32[]{:S(2)}, u32[]{:S(2)}) %all-to-all-start) | async-done | bytes 16777248 | tf_op jit(solution)/shard_map/all_to_all | solution.py:57
  740.4 17.1 %copy.24 = bf16[64,2,512,128]{3,1,0,2:T(2,128)(2,1)S(1)} copy(bf16[64,2,512,128]{3,1,2,0:T(2,128)(2,1)} %all-to-all-done) | data formatting | bytes 33554432 | tf_op jit(solution)/shard_map/all_to_all | solution.py:57
  757.5 3.0 fusion.27
  762.6 13.0 %all-reduce.1 = (f32[512]{0:T(512)S(1)}, f32[512]{0:T(512)S(1)}, f32[512]{0:T(512)S(1)}) all-reduce(f32[512]{0:T(512)S(1)} %get-tuple-element.11, f32[512]{0:T(512)S(1)} %get-tuple-element.22, f32[512]{0:T(512)S(1)} %get-tuple-element.10), channel_id=1, replica_groups=mesh['pos'=2,'tv'=8,'sv'=8] {'sv'}, use_global_device_ids=true, to_apply=%region_18.19 | all-reduce | flops 1536 | bytes 12288 | tf_op jit(solution)/shard_map/psum | solution.py:89
  775.6 24.0 %all-reduce.2 = (f32[512]{0:T(512)S(1)}, f32[512]{0:T(512)S(1)}, f32[512]{0:T(512)S(1)}) all-reduce(f32[512]{0:T(512)S(1)} %get-tuple-element.14, f32[512]{0:T(512)S(1)} %get-tuple-element.15, f32[512]{0:T(512)S(1)} %get-tuple-element.16), channel_id=1, replica_groups=mesh['pos'=2,'tv'=8,'sv'=8] {'tv'}, use_global_device_ids=true, to_apply=%region_19.20 | all-reduce | flops 1536 | bytes 12288 | tf_op jit(solution)/shard_map/psum | solution.py:88
  799.6 4.0 fusion.15
  804.2 36.6 %all-gather.2.cloned.1.call-done = bf16[1024,1024]{1,0:T(8,128)(2,1)} async-done(((bf16[512,1024]{1,0:T(8,128)(2,1)}), bf16[1024,1024]{1,0:T(8,128)(2,1)}) %all-gather.2.cloned.1.call-update) | async-done | bytes 2097168 | tf_op jit(solution)/shard_map/all_gather | solution.py:96
  840.8 9.4 %convert_bitcast_fusion = bf16[2048,1024]{0,1:T(8,128)(2,1)} fusion(bf16[1024,1024]{1,0:T(8,128)(2,1)} %all-gather.2.cloned.1.call-done, bf16[1024,2048]{1,0:T(8,128)(2,1)} %param.14), kind=kOutput, calls=%fused_computation.11 | convolution fusion | flops 4297064448 | bytes 10485760 | tf_op jit(solution)/shard_map/dot_general | solution.py:94
  850.3 6.4 copy.26
  (41 shorter events, 16.4 us)
Async XLA Ops:
  7.2 428.7 %copy-start = (bf16[48,128,128]{2,1,0:T(8,128)(2,1)S(1)}, bf16[48,128,128]{2,1,0:T(8,128)(2,1)}, u32[]{:S(2)}) copy-start(bf16[48,128,128]{2,1,0:T(8,128)(2,1)} %param.13) | copy-start | bytes 4718596
  7.2 72.1 %reduce-scatter.5.cloned.1.call-start = ((), (), s32[]{:S(2)}) async-start(), calls=%async_computation.5 | async-start | bytes 6291456 | tf_op jit(solution)/shard_map/reduce_scatter | solution.py:77
  17.3 0.7 copy-start.4
  17.3 133.6 %reduce-scatter.3.cloned.1.call-start = ((), (), s32[]{:S(2)}) async-start(), calls=%async_computation.4 | async-start | bytes 7864320 | tf_op jit(solution)/shard_map/reduce_scatter | solution.py:26
  56.1 0.7 copy-start.5
  56.1 12.9 %copy-start.6 = (s32[48]{0:T(128)S(1)}, s32[48]{0:T(128)}, u32[]{:S(2)}) copy-start(s32[48]{0:T(128)} %param.11) | copy-start | bytes 580
  58.5 438.3 %all-to-all-start.1 = ((s32[64,1,2]{2,1,0:T(1,128)}), s32[64,1,2]{2,1,0:T(1,128)S(1)}, u32[]{:S(2)}, u32[]{:S(2)}) async-start(s32[64,1,2]{2,1,0:T(1,128)} %bitcast.4), calls=%async_computation.2 | async-start | bytes 65536 | tf_op jit(solution)/shard_map/all_to_all | solution.py:64
  496.7 243.6 %all-to-all-start = ((bf16[64,2,512,128]{3,1,2,0:T(2,128)(2,1)}), bf16[64,2,512,128]{3,1,2,0:T(2,128)(2,1)}, u32[]{:S(2)}, u32[]{:S(2)}) async-start(bf16[64,2,512,128]{3,1,2,0:T(2,128)(2,1)} %copy.23), calls=%async_computation.1 | async-start | bytes 33554432 | tf_op jit(solution)/shard_map/all_to_all | solution.py:57
  514.0 326.8 %all-gather.2.cloned.1.call-start = ((), (), s32[]{:S(2)}) async-start(), calls=%async_computation.6 | async-start | bytes 3145728 | tf_op jit(solution)/shard_map/all_gather | solution.py:96
  757.5 4.4 copy-start.3
  760.5 1.3 copy-start.2
  840.8 15.8 %copy-start.1 = (bf16[48,128,128]{2,1,0:T(8,128)(2,1)S(1)}, bf16[48,128,128]{2,1,0:T(8,128)(2,1)}, u32[]{:S(2)}) copy-start(bf16[48,128,128]{2,1,0:T(8,128)(2,1)} %param.13) | copy-start | bytes 4718596
Sparse Core Ops, SparseCore 0:
  17.4 61.8 reduce-scatter.4
  81.7 69.1 reduce-scatter.2
  803.7 37.0 all-gather.1
